TPU v7x, 32 devices: a whole 2x2x4 slice. The times are simulated.
32 devices in a mesh: op: 4 (over z), sec: 8 (over y, x, core).
Axes of the slice: x: 2, y: 2, z: 4, core: 2. Of those that a mesh axis runs over, the one named last changes fastest.
Arguments:
- state_vector: bfloat16 [512, 8, 512], P(None, 'sec'), may hold values from -6 to 6
- left_env: bfloat16 [60, 8, 512, 512], P('op', 'sec'), may hold values from -0.25 to 0.25
- right_env: bfloat16 [60, 8, 512, 512], P('op', 'sec'), may hold values from -0.03125 to 0.03125
- op_shift: int32 [60, 2], P('op'), may hold values from -1 to 1, as said below
- sector_charge: int32 [8, 2], replicated, may hold values from 0 to 3, as said below
Outputs:
- hpsi: bfloat16 [512, 8, 512], P('op', 'sec')
Inputs may be any that keep to these rules, and one draw needn't show every extreme that they name: `sector_charge`: row n holds the charges of the sector in slot n; the rows are the 2 x 4 pairs (up below 2, down below 4), each once. `op_shift`: each operator changes at most one of the two charges.
All inputs are finite; a program needn't handle non-finite values.
Results may differ from a plain program's by a relative error of at most 0.0049.
Values may be sent and summed in bfloat16 or wider, within the bound.
No kernel may reach another device: no remote copies, remote signals or barrier semaphores. Data moves between devices by JAX's collectives and lax.ppermute only.
A program may use at most 128 MiB of HBM per device.

v0:
```python
import jax
import jax.numpy as jnp
from jax import lax
from jax.sharding import PartitionSpec as P


def find_sources(own_charge, all_charge, op_shift):
    target = own_charge[None, :, :] - op_shift[:, None, :]
    matches = jnp.all(target[:, :, None, :] == all_charge[None, None, :, :], axis=-1)
    slot_ids = jnp.arange(all_charge.shape[0], dtype=jnp.int32)
    source_slot = jnp.sum(jnp.where(matches, slot_ids, 0), axis=-1)
    present = jnp.any(matches, axis=-1)
    return (source_slot, present)


def on_device(state_vector, left_env, right_env, op_shift, sector_charge):
    sec_count = left_env.shape[1]
    gathered = lax.all_gather(state_vector, "sec", axis=1, tiled=True)
    own_charge = lax.dynamic_slice_in_dim(
        sector_charge, lax.axis_index("sec") * sec_count, sec_count, 0
    )
    source_slot, present = find_sources(own_charge, sector_charge, op_shift)
    sources = jnp.take(gathered, source_slot, axis=1)
    sources = jnp.where(present[None, :, :, None], sources, jnp.zeros((), sources.dtype))
    halfway = jnp.einsum(
        "bgij,jbgk->bgik", left_env, sources, preferred_element_type=jnp.float32
    ).astype(jnp.bfloat16)
    summed = lax.psum_scatter(
        jnp.einsum("bgik,bglk->igl", halfway, right_env, preferred_element_type=jnp.float32),
        "op",
        scatter_dimension=0,
        tiled=True,
    )
    return summed.astype(jnp.bfloat16)


def solution(mesh):
    placed = (
        P(None, "sec", None),
        P("op", "sec", None, None),
        P("op", "sec", None, None),
        P("op", None),
        P(),
    )
    return jax.shard_map(
        on_device, mesh=mesh, in_specs=placed, out_specs=P("op", "sec", None), check_vma=False
    )
```

profile of v0, /device:TPU:0, one launch (start us, length us, event | category | flops | bytes accessed | tf_op | source)
XLA Modules:
  0.0 105.2 jit_solution(13239044348452605065)
XLA Ops:
  6.5 0.0 all-gather.2.cloned.1.call-start
  6.5 0.7 all-gather.2.cloned.1.call-update
  7.3 0.0 reduce-scatter.2.cloned.1.call-start
  7.3 0.9 dynamic-slice_reduce_fusion
  8.2 0.8 broadcast_subtract_fusion
  8.9 0.8 compare_reduce_fusion
  9.8 38.9 %all-gather.2.cloned.1.call-done = bf16[512,8,512]{2,0,1:T(8,128)(2,1)} async-done(((bf16[512,1,512]{2,0,1:T(8,128)(2,1)}), bf16[512,8,512]{2,0,1:T(8,128)(2,1)}) %all-gather.2.cloned.1.call-update) | async-done | bytes 4194320 | tf_op jit(solution)/shard_map/all_gather | solution.py:18
  48.7 6.6 %gather_fusion = bf16[15,512,512]{2,1,0:T(8,128)(2,1)} fusion(bf16[512,8,512]{2,0,1:T(8,128)(2,1)} %all-gather.2.cloned.1.call-done, s32[1024]{0:T(1024)S(1)} %pad_clamp_fusion), kind=kCustom, calls=%fused_computation | custom fusion | bytes 15728700 | tf_op jit(solution)/shard_map/jit(_take)/gather | solution.py:23
  55.3 14.0 %fusion.24 = f32[512,1,512]{2,0,1:T(8,128)} fusion(bf16[15,1,512,512]{3,2,1,0:T(8,128)(2,1)} %param.7, bf16[15,1,512,512]{3,2,1,0:T(8,128)(2,1)} %param.6, bf16[15,512,512]{2,1,0:T(8,128)(2,1)} %gather_fusion, pred[15]{0:T(512)(128)(4,1)S(1)} %reduce_or.9, pred[15]{0:T(512)(128)(4,1)S(1)} %compare_and_fusion), kind=kOutput, calls=%fused_computation.14 | convolution fusion | flops 8064860160 | bytes 24641566 | tf_op jit(solution)/shard_map/bgik,bglk->igl/dot_general | solution.py:29
  69.3 0.0 reduce-scatter.2.cloned.1.call-update
  69.4 27.4 %reduce-scatter.2.cloned.1.call-done = f32[128,1,512]{2,0,1:T(8,128)} async-done(((f32[512,1,512]{2,0,1:T(8,128)}), f32[128,1,512]{2,0,1:T(8,128)}) %reduce-scatter.2.cloned.1.call-update) | async-done | bytes 262160 | tf_op jit(solution)/shard_map/reduce_scatter | solution.py:28
  96.8 1.6 %convert_element_type.12 = bf16[128,1,512]{2,0,1:T(8,128)(2,1)} convert(f32[128,1,512]{2,0,1:T(8,128)} %reduce-scatter.2.cloned.1.call-done) | non-fusion elementwise | flops 65536 | bytes 393216 | tf_op jit(solution)/shard_map/convert_element_type | solution.py:34
  (5 shorter events, 0.1 us)
Async XLA Ops:
  6.5 42.2 %all-gather.2.cloned.1.call-start = ((), (), s32[]{:S(2)}) async-start(), calls=%async_computation.1 | async-start | bytes 4718592 | tf_op jit(solution)/shard_map/all_gather | solution.py:18
  7.3 89.5 %reduce-scatter.2.cloned.1.call-start = ((), (), s32[]{:S(2)}) async-start(), calls=%async_computation.2 | async-start | bytes 1310720 | tf_op jit(solution)/shard_map/reduce_scatter | solution.py:28
Sparse Core Ops, SparseCore 0:
  9.2 39.4 all-gather.1
  69.5 27.2 reduce-scatter.1
where the time goes:
time: 105 us
  waiting for transfers between devices  67.1 us (64%)
  matrix products  14 us (13%)
  between operations  13.4 us (13%)
  local copies, waits for them, and re-layouts  7.49 us (7%)
  other arithmetic  3.19 us (3%)
    all_gather x1, waiting for transfers between devices, on_device(): gathered = lax.all_gather(state_vector, 'sec', axis=1, tiled=True)  38.9 us
    reduce_scatter x1, waiting for transfers between devices, on_device(): lax.psum_scatter(jnp.einsum('bgik,bglk->igl', halfway, right_env, preferr...  27.4 us
    dot_general x1, matrix products, on_device(): jnp.einsum('bgik,bglk->igl', halfway, right_env, preferred_element_type=j...  14 us
    gather x1, local copies, waits for them, and re-layouts, on_device(): sources = jnp.take(gathered, source_slot, axis=1)  6.63 us
  transfers between devices with their start and end apart: 2, of which 2 were waited for; matrix products, arithmetic and copies ran while one was open for 2% of the time, Pallas kernels for 0%

commit v1 on v0

v1 whole, which is shorter than its diff:
```python
import functools

import jax
import jax.numpy as jnp
from jax import lax
from jax.experimental import pallas as pl
from jax.experimental.pallas import tpu as pltpu
from jax.sharding import PartitionSpec as P

SIDE = 6
LIMIT = 6
SMEM = pl.BlockSpec(memory_space=pltpu.SMEM)
VMEM = pl.BlockSpec(memory_space=pltpu.VMEM)
HBM = pl.BlockSpec(memory_space=pltpu.HBM)
ANY = pl.BlockSpec(memory_space=pl.ANY)


def find_positions(me, position_of, shift, charge, table, plan):
    for i in range(SIDE * SIDE):
        table[i] = -1
    for n in range(charge.shape[1]):
        table[(charge[0, n] + 1) * SIDE + charge[1, n] + 1] = n
    base = (charge[0, me] + 1) * SIDE + charge[1, me] + 1

    def visit(b, carry):
        slot = table[base - shift[0, b] * SIDE - shift[1, b]]
        plan[b] = jnp.where(slot < 0, -1, position_of(me, slot))
        return carry

    lax.fori_loop(0, shift.shape[1], visit, 0)


def list_operators(plan, order, places, skip=0):
    def visit(b, carry):
        count, seen = carry
        position = plan[b]
        index = jnp.int32(-1)
        for i, place in enumerate(places):
            index = jnp.where(position == place, i, index)
        order[0, count] = b
        order[1, count] = index
        here = index >= 0
        if skip:
            here = here & ((position != 0) | (seen >= skip))
            seen = seen + (position == 0).astype(jnp.int32)
        return count + here.astype(jnp.int32), seen

    return lax.fori_loop(0, plan.shape[0], visit, (jnp.int32(0), jnp.int32(0)))[0]


def product(left, source, right):
    halfway, begin = None, 0
    for piece in source:
        end = begin + piece.shape[0]
        term = jnp.dot(left[:, begin:end], piece[...], preferred_element_type=jnp.float32)
        halfway, begin = term if halfway is None else halfway + term, end
    halfway = halfway.astype(jnp.bfloat16)
    return lax.dot_general(halfway, right[...], (((1,), (1,)), ((), ())), preferred_element_type=jnp.float32)


def add_operators(total, count, order, left, right, source, ready):
    def term(i):
        b = order[0, i]
        ready(b)
        return left.at[b], source(order[1, i]), right.at[b]

    def pair(i, carry):
        one, two = term(2 * i), term(2 * i + 1)
        total[...] += product(*one) + product(*two)
        return carry

    lax.fori_loop(0, count // 2, pair, 0)

    @pl.when(count % 2 == 1)
    def _():
        total[...] += product(*term(count - 1))


def each(count, order, act, begin=0):
    def body(i, carry):
        act(order[0, i])
        return carry

    lax.fori_loop(begin, count, body, 0)


class Loads:
    def __init__(self, left_hbm, right_hbm, left, right, sems):
        self.refs = left_hbm, right_hbm, left, right, sems

    def both(self, b, at):
        left_hbm, right_hbm, left, right, sems = self.refs
        return (
            pltpu.make_async_copy(left_hbm.at[b], left.at[at], sems.at[0, at]),
            pltpu.make_async_copy(right_hbm.at[b], right.at[at], sems.at[1, at]),
        )

    def start(self, b, at=None):
        for copy in self.both(b, b if at is None else at):
            copy.start()

    def wait(self, b, at=None):
        for copy in self.both(b, b if at is None else at):
            copy.wait()


def load_sources(pieces, refs, source, sems):
    copies = []
    for i, sizes in enumerate(pieces):
        begin = 0
        for size in sizes:
            at = len(copies)
            copies.append(
                pltpu.make_async_copy(refs[at], source.at[i, pl.ds(begin, size)], sems.at[at])
            )
            begin += size
    for copy in copies:
        copy.start()
    return copies


def first_kernel(position_of, limit, shift_hbm, charge_hbm, left_hbm, right_hbm, own_hbm, *refs):
    total, plan, left, right, source, shift, charge, table, order, sems, small = refs
    copies = [
        pltpu.make_async_copy(shift_hbm, shift, small.at[0]),
        pltpu.make_async_copy(charge_hbm, charge, small.at[1]),
        pltpu.make_async_copy(own_hbm, source.at[0], small.at[2]),
    ]
    for copy in copies:
        copy.start()
    for copy in copies[:2]:
        copy.wait()
    find_positions(lax.axis_index("sec"), position_of, shift, charge, table, plan)
    count = jnp.minimum(list_operators(plan, order, [0]), limit)
    loads = Loads(left_hbm, right_hbm, left, right, sems)

    def start(i, carry):
        loads.start(order[0, i], i)
        order[0, i] = i
        return carry

    lax.fori_loop(0, count, start, 0)
    total[...] = jnp.zeros_like(total)
    copies[2].wait()
    add_operators(
        total, count, order, left, right, lambda at: [source.at[at]], lambda at: loads.wait(0, at)
    )


def second_kernel(pieces, places, skip, others, *refs):
    plan, left_hbm, right_hbm = refs[:3]
    n_in = sum(len(p) for p in pieces)
    inputs, rest = refs[4 : 4 + n_in], refs[4 + n_in :]
    total, left, right, source, now, later, sems, source_sems = rest
    loads = Loads(left_hbm, right_hbm, left, right, sems)
    sources = load_sources(pieces, inputs, source, source_sems)
    count = list_operators(plan, now, places, skip)
    each(count, now, loads.start)
    behind = list_operators(plan, later, others)
    each(behind, later, loads.start)
    for copy in sources:
        copy.wait()
    add_operators(total, count, now, left, right, lambda at: [source.at[at]], loads.wait)
    each(behind, later, loads.wait)


def next_kernel(counts, places, sends, plan, left, right, before, *refs):
    del before
    flat = refs[: sum(counts)]
    total, *outs, order = refs[sum(counts) :]
    begin = 0
    for n, place in zip(counts, places):
        block = flat[begin : begin + n]
        begin += n
        count = list_operators(plan, order, [place])
        add_operators(total, count, order, left, right, lambda at: block, lambda b: None)
    for out, flip in zip(outs, sends):
        rows = out.shape[0]
        at = pl.multiple_of((lax.axis_index("op") ^ flip) * rows, rows)
        out[...] = total[pl.ds(at, rows), :].astype(out.dtype)


def general_kernel(slots, *refs):
    shift, charge, left_hbm, right_hbm, blocks_hbm = refs[:5]
    total, source, left, right, plan, table, order, sems, block_sem = refs[5:]
    copy = pltpu.make_async_copy(blocks_hbm, source, block_sem)
    copy.start()
    find_positions(lax.axis_index("sec"), by_slot, shift, charge, table, plan)
    count = list_operators(plan, order, range(slots))
    loads = Loads(left_hbm, right_hbm, left, right, sems)
    each(count, order, loads.start)
    total[...] = jnp.zeros_like(total)
    copy.wait()
    add_operators(total, count, order, left, right, lambda at: [source.at[at]], loads.wait)


def cost(flops, moved):
    return pl.CostEstimate(flops=flops, bytes_accessed=moved, transcendentals=0)


def in_hbm(x):
    return pltpu.with_memory_space_constraint(x, pltpu.HBM)


def limit_vmem(mib):
    return pltpu.CompilerParams(vmem_limit_bytes=mib << 20)


def start_sum(own, position_of, limit, shift, charge, left_env, right_env):
    operators, rows, inner = left_env.shape
    columns, width = right_env.shape[1:]
    return pl.pallas_call(
        functools.partial(first_kernel, position_of, limit),
        out_shape=[
            jax.ShapeDtypeStruct((rows, columns), jnp.float32),
            jax.ShapeDtypeStruct((operators,), jnp.int32),
        ],
        in_specs=[HBM] * 5,
        out_specs=[VMEM, SMEM],
        scratch_shapes=[
            pltpu.VMEM((limit, rows, inner), jnp.bfloat16),
            pltpu.VMEM((limit, columns, width), jnp.bfloat16),
            pltpu.VMEM((1, inner, width), jnp.bfloat16),
            pltpu.SMEM(shift.shape, jnp.int32),
            pltpu.SMEM(charge.shape, jnp.int32),
            pltpu.SMEM((SIDE * SIDE,), jnp.int32),
            pltpu.SMEM((2, operators + 1), jnp.int32),
            pltpu.SemaphoreType.DMA((2, limit)),
            pltpu.SemaphoreType.DMA((3,)),
        ],
        compiler_params=limit_vmem(24),
        cost_estimate=cost(limit * 4 * rows * inner * width, limit * 4 * rows * inner),
    )(in_hbm(shift), in_hbm(charge), in_hbm(left_env), in_hbm(right_env), in_hbm(own))


def add_and_load(blocks, places, skip, others, plan, left_env, right_env, before):
    pieces = [[p.shape[0] for p in block] for block in blocks]
    flat = [p for block in blocks for p in block]
    operators, rows, inner = left_env.shape
    columns, width = right_env.shape[1:]
    return pl.pallas_call(
        functools.partial(second_kernel, pieces, places, skip, others),
        out_shape=[
            jax.ShapeDtypeStruct(before.shape, jnp.float32),
            jax.ShapeDtypeStruct(left_env.shape, left_env.dtype),
            jax.ShapeDtypeStruct(right_env.shape, right_env.dtype),
        ],
        in_specs=[SMEM, HBM, HBM, VMEM] + [ANY] * len(flat),
        out_specs=[VMEM] * 3,
        input_output_aliases={3: 0},
        scratch_shapes=[
            pltpu.VMEM((len(blocks), inner, width), jnp.bfloat16),
            pltpu.SMEM((2, operators + 1), jnp.int32),
            pltpu.SMEM((2, operators + 1), jnp.int32),
            pltpu.SemaphoreType.DMA((2, operators)),
            pltpu.SemaphoreType.DMA((len(flat),)),
        ],
        compiler_params=limit_vmem(24),
        cost_estimate=cost(operators * 2 * rows * inner * width, operators * 4 * rows * inner),
    )(plan, in_hbm(left_env), in_hbm(right_env), before, *flat)


def add_blocks(blocks, places, sends, ops, plan, left, right, before):
    flat = [p for block in blocks for p in block]
    operators, rows, inner = left.shape
    columns, width = right.shape[1:]
    return pl.pallas_call(
        functools.partial(next_kernel, [len(block) for block in blocks], places, sends),
        out_shape=[jax.ShapeDtypeStruct((rows, columns), jnp.float32)]
        + [
            jax.ShapeDtypeStruct((rows // ops, columns), jnp.bfloat16 if flip else jnp.float32)
            for flip in sends
        ],
        in_specs=[SMEM] + [VMEM] * (3 + len(flat)),
        out_specs=[VMEM] * (1 + len(sends)),
        scratch_shapes=[pltpu.SMEM((2, operators + 1), jnp.int32)],
        input_output_aliases={3: 0},
        compiler_params=limit_vmem(16),
        cost_estimate=cost(operators * rows * inner * width, operators * rows * inner),
    )(plan, left, right, before, *flat)


def sum_all(blocks, shift, charge, left_env, right_env):
    operators, rows, inner = left_env.shape
    columns, width = right_env.shape[1:]
    return pl.pallas_call(
        functools.partial(general_kernel, blocks.shape[0]),
        out_shape=jax.ShapeDtypeStruct((rows, columns), jnp.float32),
        in_specs=[SMEM, SMEM] + [HBM] * 3,
        out_specs=VMEM,
        scratch_shapes=[
            pltpu.VMEM(blocks.shape, blocks.dtype),
            pltpu.VMEM(left_env.shape, left_env.dtype),
            pltpu.VMEM(right_env.shape, right_env.dtype),
            pltpu.SMEM((operators,), jnp.int32),
            pltpu.SMEM((SIDE * SIDE,), jnp.int32),
            pltpu.SMEM((2, operators + 1), jnp.int32),
            pltpu.SemaphoreType.DMA((2, operators)),
            pltpu.SemaphoreType.DMA,
        ],
        compiler_params=limit_vmem(48),
        cost_estimate=cost(operators * 4 * rows * inner * width, operators * 4 * rows * inner),
    )(shift, charge, left_env, right_env, blocks)


def by_slot(me, slot):
    return slot


def by_arrival(me, slot):
    flip = slot ^ me
    turned = ((me ^ lax.axis_index("op")) & 1) == 1
    return jnp.where(turned & (flip >= 2) & (flip < 6), flip ^ 6, flip)


def on_eight(ops, op_shift, sector_charge, own, left_env, right_env):
    secs = 8
    axes = ("op", "sec")
    devices = [(z, s) for z in range(ops) for s in range(secs)]

    def pairs(move):
        return [(z * secs + s, (lambda t: t[0] * secs + t[1])(move(z, s))) for z, s in devices]

    first_flip = lambda z, s: 2 if (z + s) % 2 == 0 else 4
    to_first = pairs(lambda z, s: (z, s ^ first_flip(z, s)))
    to_second = pairs(lambda z, s: (z, s ^ 6 ^ first_flip(z, s)))
    to_core = pairs(lambda z, s: (z, s ^ 1))
    to_plane = pairs(lambda z, s: (z ^ 1, s))
    cut = own.shape[0] // 2
    barrier = lax.optimization_barrier
    later = (3, 4, 6, 7)

    first = lax.ppermute(own, axes, to_first)
    second_bottom = lax.ppermute(own[cut:], axes, to_second)
    other = lax.ppermute(own, axes, to_core)
    total, plan = start_sum(
        own, by_arrival, LIMIT, op_shift.T, sector_charge.T, left_env, right_env
    )
    first, total = barrier((first, total))
    second_top = lax.ppermute(first[:cut], axes, to_plane)
    far = lax.ppermute(first, axes, to_second)
    other_first = lax.ppermute(first, axes, to_core)
    total, left, right = add_and_load(
        [[own], [other], [first], [other_first]], (0, 1, 2, 5), LIMIT, later,
        plan, left_env, right_env, total,
    )
    second_bottom, total = barrier((second_bottom, total))
    other_second_bottom = lax.ppermute(second_bottom, axes, to_core)
    add = functools.partial(add_blocks, ops=ops, plan=plan, left=left, right=right)
    second_top, far, total = barrier((second_top, far, total))
    other_second_top = lax.ppermute(second_top, axes, to_core)
    other_far = lax.ppermute(far, axes, to_core)
    (total,) = add([[second_top, second_bottom], [far]], (4, 6), (), before=total)
    _, *parts = add(
        [[other_second_top, other_second_bottom], [other_far]], (3, 7), tuple(range(ops)),
        before=total,
    )
    result = parts[0]
    for flip in (3, 2, 1):
        sent = lax.ppermute(parts[flip], "op", [(i, i ^ flip) for i in range(ops)])
        result = result + sent.astype(jnp.float32)
    return result


def on_any(secs, ops, op_shift, sector_charge, own, left_env, right_env):
    gathered = lax.all_gather(own, "sec", axis=0)
    total = sum_all(gathered, op_shift.T, sector_charge.T, left_env, right_env)
    rows = total.shape[0] // ops
    me = lax.axis_index("op")
    part = lambda flip: lax.dynamic_slice_in_dim(total, (me ^ flip) * rows, rows, 0)
    result = part(0)
    for flip in range(1, ops):
        sent = part(flip).astype(jnp.bfloat16)
        sent = lax.ppermute(sent, "op", [(i, i ^ flip) for i in range(ops)])
        result = result + sent.astype(jnp.float32)
    return result


def on_device(secs, ops, state_vector, left_env, right_env, op_shift, sector_charge):
    own = state_vector.reshape(state_vector.shape[0], state_vector.shape[2])
    left_env = left_env.reshape(left_env.shape[0], *left_env.shape[2:])
    right_env = right_env.reshape(right_env.shape[0], *right_env.shape[2:])
    apply = (
        functools.partial(on_eight, ops)
        if secs == 8 and ops == 4
        else functools.partial(on_any, secs, ops)
    )
    hpsi = apply(op_shift, sector_charge, own, left_env, right_env)
    return hpsi.astype(jnp.bfloat16)[:, None, :]


def solution(mesh):
    placed = (
        P(None, "sec", None),
        P("op", "sec", None, None),
        P("op", "sec", None, None),
        P("op", None),
        P(),
    )
    return jax.shard_map(
        functools.partial(on_device, mesh.shape["sec"], mesh.shape["op"]),
        mesh=mesh,
        in_specs=placed,
        out_specs=P("op", "sec", None),
        check_vma=False,
    )
```

time: 105 us -> 43.2 us (0.41)
  waiting for transfers between devices: 67.1 us -> 12.8 us
  Pallas kernels: 0 us -> 17.5 us
  matrix products: 14 us -> 0 us
  between operations: 13.4 us -> 0.09 us
  starting transfers between devices: 0.04 us -> 12.2 us
  local copies, waits for them, and re-layouts: 7.49 us -> 0.04 us
  other arithmetic: 3.19 us -> 0.72 us
    all_gather x1 -> x0, waiting for transfers between devices: 38.9 us -> none  [on_device(): gathered = lax.all_gather(state_vector, 'sec', axis=1, tiled=True)]
    reduce_scatter x1 -> x0, waiting for transfers between devices: 27.4 us -> none  [on_device(): lax.psum_scatter(jnp.einsum('bgik,bglk->igl', halfway, right_env, preferr...]
    pallas_call x0 -> x4, Pallas kernels: none -> 17.5 us  [the longest x2 6.82 us: add_blocks(): pl.pallas_call(functools.partial(next_kernel, [len(block) for block in bl...]
    dot_general x1 -> x0, matrix products: 14 us -> none  [on_device(): jnp.einsum('bgik,bglk->igl', halfway, right_env, preferred_element_type=j...]
    ppermute x0 -> x12, waiting for transfers between devices: none -> 12.8 us  [the longest x3 8.44 us: on_eight(): sent = lax.ppermute(parts[flip], 'op', [(i, i ^ flip) for i in range(ops)])]
    ppermute x0 -> x12, starting transfers between devices: none -> 12.2 us  [the longest x3 4.45 us: on_eight(): sent = lax.ppermute(parts[flip], 'op', [(i, i ^ flip) for i in range(ops)])]
    gather x1 -> x0, local copies, waits for them, and re-layouts: 6.63 us -> none  [on_device(): sources = jnp.take(gathered, source_slot, axis=1)]
    convert_element_type x1 -> x0, other arithmetic: 1.62 us -> none  [on_device(): return summed.astype(jnp.bfloat16)]
  transfers between devices with their start and end apart: 2 -> 12, of which waited for: 2 -> 4; matrix products, arithmetic and copies ran while one was open for 2% -> 0% of each run, Pallas kernels for 0% -> 32%
where the time goes in v1:
time: 43.2 us; the launch traced here: 43.4 us
  Pallas kernels  17.5 us (41%)
  waiting for transfers between devices  12.8 us (30%)
  starting transfers between devices  12.2 us (28%)
  other arithmetic  0.72 us (2%)
    ppermute x3, waiting for transfers between devices, on_eight(): sent = lax.ppermute(parts[flip], 'op', [(i, i ^ flip) for i in range(ops)])  8.44 us
    pallas_call x2, Pallas kernels, add_blocks(): pl.pallas_call(functools.partial(next_kernel, [len(block) for block in bl...  6.82 us
    pallas_call x1, Pallas kernels, start_sum(): pl.pallas_call(functools.partial(first_kernel, position_of, limit), out_s...  5.98 us
    pallas_call x1, Pallas kernels, add_and_load(): pl.pallas_call(functools.partial(second_kernel, pieces, places, skip, oth...  4.72 us
    ppermute x3, starting transfers between devices, on_eight(): sent = lax.ppermute(parts[flip], 'op', [(i, i ^ flip) for i in range(ops)])  4.45 us
    ppermute x1, waiting for transfers between devices, on_eight(): second_bottom = lax.ppermute(own[cut:], axes, to_second)  2.97 us
    ppermute x1, starting transfers between devices, on_eight(): first = lax.ppermute(own, axes, to_first)  2.94 us
    ppermute x1, starting transfers between devices, on_eight(): second_top = lax.ppermute(first[:cut], axes, to_plane)  2.13 us
  transfers between devices with their start and end apart: 12, of which 4 were waited for; matrix products, arithmetic and copies ran while one was open for 0% of the time, Pallas kernels for 32%

profile of v1, /device:TPU:0, one launch (start us, length us, event | category | flops | bytes accessed | tf_op | source)
XLA Modules:
  0.0 43.4 jit_solution(3983922433223904353)
XLA Ops:
  0.0 2.9 %collective-permute-start = (bf16[512,512]{1,0:T(8,128)(2,1)}, bf16[512,512]{1,0:T(8,128)(2,1)S(1)}, u32[]{:S(2)}, u32[]{:S(2)}) collective-permute-start(bf16[512,512]{1,0:T(8,128)(2,1)} %bitcast.9), channel_id=1, source_target_pairs={{0,2},{1,5},{2,0},{3,7},{4,6},{5,1},{6,4},{7,3},{8,12},{9,11},{10,... | collective-permute-start | bytes 1572872 | tf_op jit(solution)/shard_map/ppermute | solution.py:333
  2.9 0.0 collective-permute-start.1
  2.9 0.0 copy-start
  2.9 6.0 %shard_map.55 = (f32[512,512]{1,0:T(8,128)S(1)}, s32[15]{0:T(128)S(1)}) custom-call(s32[2,15]{1,0:T(2,128)} %bitcast.17, s32[2,8]{1,0:T(2,128)} %bitcast.18, bf16[15,512,512]{2,1,0:T(8,128)(2,1)} %bitcast.13, bf16[15,512,512]{2,1,0:T(8,128)(2,1)} %bitcast.15, bf16[512,512]{1,0:T(8,128)(2,1)} %bitcast.11), custom_call_target="tpu_custom_call" | custom-call | flops 3221225472 | bytes 6291456 | tf_op jit(solution)/shard_map/pallas_call | solution.py:212
  8.9 1.4 %collective-permute-done.refs_6_ = bf16[512,512]{1,0:T(8,128)(2,1)S(1)} collective-permute-done((bf16[512,512]{1,0:T(8,128)(2,1)}, bf16[512,512]{1,0:T(8,128)(2,1)S(1)}, u32[]{:S(2)}, u32[]{:S(2)}) %collective-permute-start) | collective-permute-done | bytes 524320 | tf_op jit(solution)/shard_map/ppermute | solution.py:333
  10.3 0.0 collective-permute-start.2
  10.3 2.1 %collective-permute-start.4 = (bf16[512,512]{1,0:T(8,128)(2,1)S(1)}, bf16[512,512]{1,0:T(8,128)(2,1)S(1)}, u32[]{:S(2)}, u32[]{:S(2)}) collective-permute-start(bf16[512,512]{1,0:T(8,128)(2,1)S(1)} %collective-permute-done.refs_6_), channel_id=1, source_target_pairs={{0,4},{1,3},{2,6},{3,1},{4,0},{5,7},{6,2},{7,5},{8,10},{9,13},{10,... | collective-permute-start | bytes 1572872 | tf_op jit(solution)/shard_map/ppermute | solution.py:341
  12.4 0.0 copy-done
  12.4 0.1 collective-permute-start.5
  12.5 2.1 %collective-permute-start.3 = (bf16[256,512]{1,0:T(8,128)(2,1)S(1)}, bf16[256,512]{1,0:T(8,128)(2,1)S(1)}, u32[]{:S(2)}, u32[]{:S(2)}) collective-permute-start(bf16[256,512]{1,0:T(8,128)(2,1)S(1)} %slice.9), channel_id=1, source_target_pairs={{0,8},{1,9},{2,10},{3,11},{4,12},{5,13},{6,14},{7,15},{8,0},{9,1},... | collective-permute-start | bytes 786440 | tf_op jit(solution)/shard_map/ppermute | solution.py:340
  14.6 0.0 collective-permute-done.1.refs_5_
  14.6 0.0 collective-permute-done.2.refs_7_
  14.6 4.7 %shard_map.56 = (f32[512,512]{1,0:T(8,128)S(1)}, bf16[15,512,512]{2,1,0:T(8,128)(2,1)S(1)}, bf16[15,512,512]{2,1,0:T(8,128)(2,1)S(1)}) custom-call(s32[15]{0:T(128)S(1)} %get-tuple-element.21.refs_0_.plan, bf16[15,512,512]{2,1,0:T(8,128)(2,1)} %bitcast.14, bf16[15,512,512]{2,1,0:T(8,128)(2,1)} %bitcast.16, ...), custom_call_target="tpu_custom_call", output_to_operand_aliasing={{0}: (3, {})} | custom-call | flops 4026531840 | bytes 15728640 | tf_op jit(solution)/shard_map/pallas_call | solution.py:241
  19.4 3.0 %collective-permute-done.5.refs_1_ = bf16[256,512]{1,0:T(8,128)(2,1)S(1)} collective-permute-done((bf16[256,512]{1,0:T(8,128)(2,1)S(1)}, bf16[256,512]{1,0:T(8,128)(2,1)S(1)}, u32[]{:S(2)}, u32[]{:S(2)}) %collective-permute-start.5) | collective-permute-done | bytes 262176 | tf_op jit(solution)/shard_map/ppermute | solution.py:334
  22.3 0.0 collective-permute-done.3.refs_0_
  22.3 0.0 collective-permute-done.4.refs_2_
  22.3 0.0 collective-permute-start.8
  22.3 0.5 %collective-permute-start.6 = (bf16[256,512]{1,0:T(8,128)(2,1)S(1)}, bf16[256,512]{1,0:T(8,128)(2,1)S(1)}, u32[]{:S(2)}, u32[]{:S(2)}) collective-permute-start(bf16[256,512]{1,0:T(8,128)(2,1)S(1)} %collective-permute-done.3.refs_0_), channel_id=1, source_target_pairs={{0,1},{1,0},{2,3},{3,2},{4,5},{5,4},{6,7},{7,6},{8,9},{9,8},{10,11... | collective-permute-start | bytes 786440 | tf_op jit(solution)/shard_map/ppermute | solution.py:351
  22.9 0.1 collective-permute-start.7
  22.9 3.3 %shard_map.57.before = f32[512,512]{1,0:T(8,128)S(1)} custom-call(s32[15]{0:T(128)S(1)} %get-tuple-element.21.refs_0_.plan, bf16[15,512,512]{2,1,0:T(8,128)(2,1)S(1)} %get-tuple-element.25.left, bf16[15,512,512]{2,1,0:T(8,128)(2,1)S(1)} %get-tuple-element.26.right, f32[512,512]{1,0:T(8,128)S(1)} %get-tuple-element.29.before, ...), custom_call_target="tpu_custom_call", output_to_operand_aliasing={{}: (3, {})} | custom-call | flops 2013265920 | bytes 3932160 | tf_op jit(solution)/shard_map/pallas_call | solution.py:267
  26.2 0.0 collective-permute-done.6.refs_0_
  26.2 0.0 collective-permute-done.7.refs_1_
  26.2 0.0 collective-permute-done.8.refs_2_
  26.3 3.5 %shard_map.58 = (f32[512,512]{1,0:T(8,128)S(1)}, f32[128,512]{1,0:T(8,128)S(1)}, bf16[128,512]{1,0:T(8,128)(2,1)S(1)}, bf16[128,512]{1,0:T(8,128)(2,1)S(1)}, bf16[128,512]{1,0:T(8,128)(2,1)S(1)}) custom-call(s32[15]{0:T(128)S(1)} %get-tuple-element.21.refs_0_.plan, ...), custom_call_target="tpu_custom_call", output_to_operand_aliasing={{0}: (3, {})} | custom-call | flops 2013265920 | bytes 3932160 | tf_op jit(solution)/shard_map/pallas_call | solution.py:267
  29.8 1.2 %collective-permute-start.10 = (bf16[128,512]{1,0:T(8,128)(2,1)S(1)}, bf16[128,512]{1,0:T(8,128)(2,1)S(1)}, u32[]{:S(2)}, u32[]{:S(2)}) collective-permute-start(bf16[128,512]{1,0:T(8,128)(2,1)S(1)} %get-tuple-element.35), channel_id=1, source_target_pairs={{0,16},{8,24},{16,0},{24,8},{1,17},{9,25},{17,1},{25,9},{2,18},{10... | collective-permute-start | bytes 393224 | tf_op jit(solution)/shard_map/ppermute | solution.py:360
  31.0 2.1 %collective-permute-start.11 = (bf16[128,512]{1,0:T(8,128)(2,1)S(1)}, bf16[128,512]{1,0:T(8,128)(2,1)S(1)}, u32[]{:S(2)}, u32[]{:S(2)}) collective-permute-start(bf16[128,512]{1,0:T(8,128)(2,1)S(1)} %get-tuple-element.36), channel_id=1, source_target_pairs={{0,8},{8,0},{16,24},{24,16},{1,9},{9,1},{17,25},{25,17},{2,10},{10... | collective-permute-start | bytes 393224 | tf_op jit(solution)/shard_map/ppermute | solution.py:360
  33.1 1.1 %collective-permute-start.9 = (bf16[128,512]{1,0:T(8,128)(2,1)S(1)}, bf16[128,512]{1,0:T(8,128)(2,1)S(1)}, u32[]{:S(2)}, u32[]{:S(2)}) collective-permute-start(bf16[128,512]{1,0:T(8,128)(2,1)S(1)} %get-tuple-element.34), channel_id=1, source_target_pairs={{0,24},{8,16},{16,8},{24,0},{1,25},{9,17},{17,9},{25,1},{2,26},{10... | collective-permute-start | bytes 393224 | tf_op jit(solution)/shard_map/ppermute | solution.py:360
  34.2 5.9 %collective-permute-done.10 = bf16[128,512]{1,0:T(8,128)(2,1)S(1)} collective-permute-done((bf16[128,512]{1,0:T(8,128)(2,1)S(1)}, bf16[128,512]{1,0:T(8,128)(2,1)S(1)}, u32[]{:S(2)}, u32[]{:S(2)}) %collective-permute-start.10) | collective-permute-done | bytes 131104 | tf_op jit(solution)/shard_map/ppermute | solution.py:360
  40.1 2.6 %collective-permute-done.11 = bf16[128,512]{1,0:T(8,128)(2,1)S(1)} collective-permute-done((bf16[128,512]{1,0:T(8,128)(2,1)S(1)}, bf16[128,512]{1,0:T(8,128)(2,1)S(1)}, u32[]{:S(2)}, u32[]{:S(2)}) %collective-permute-start.11) | collective-permute-done | bytes 131104 | tf_op jit(solution)/shard_map/ppermute | solution.py:360
  42.7 0.0 collective-permute-done.9
  42.7 0.7 %fusion = bf16[128,1,512]{2,0,1:T(8,128)(2,1)} fusion(bf16[128,512]{1,0:T(8,128)(2,1)S(1)} %collective-permute-done.11, bf16[128,512]{1,0:T(8,128)(2,1)S(1)} %collective-permute-done.10, f32[128,512]{1,0:T(8,128)S(1)} %get-tuple-element.33, bf16[128,512]{1,0:T(8,128)(2,1)S(1)} %collective-permute-done.9), kind=kLoop, calls=%fused_computation.2 | loop fusion | flops 458752 | bytes 786432 | tf_op jit(solution)/shard_map/broadcast_in_dim | solution.py:389
  (2 shorter events, 0.0 us)
Async XLA Ops:
  0.0 10.3 %collective-permute-start = (bf16[512,512]{1,0:T(8,128)(2,1)}, bf16[512,512]{1,0:T(8,128)(2,1)S(1)}, u32[]{:S(2)}, u32[]{:S(2)}) collective-permute-start(bf16[512,512]{1,0:T(8,128)(2,1)} %bitcast.9), channel_id=1, source_target_pairs={{0,2},{1,5},{2,0},{3,7},{4,6},{5,1},{6,4},{7,3},{8,12},{9,11},{10,... | collective-permute-start | bytes 1572872 | tf_op jit(solution)/shard_map/ppermute | solution.py:333
  2.9 11.7 %collective-permute-start.1 = (bf16[512,512]{1,0:T(8,128)(2,1)}, bf16[512,512]{1,0:T(8,128)(2,1)S(1)}, u32[]{:S(2)}, u32[]{:S(2)}) collective-permute-start(bf16[512,512]{1,0:T(8,128)(2,1)} %bitcast.10), channel_id=1, source_target_pairs={{0,1},{1,0},{2,3},{3,2},{4,5},{5,4},{6,7},{7,6},{8,9},{9,8},{10,11... | collective-permute-start | bytes 1572872 | tf_op jit(solution)/shard_map/ppermute | solution.py:335
  2.9 9.4 %copy-start = (bf16[512,1,512]{2,0,1:T(8,128)(2,1)S(1)}, bf16[512,1,512]{2,0,1:T(8,128)(2,1)}, u32[]{:S(2)}) copy-start(bf16[512,1,512]{2,0,1:T(8,128)(2,1)} %param.5) | copy-start | bytes 1572868
  10.3 4.3 %collective-permute-start.2 = (bf16[512,512]{1,0:T(8,128)(2,1)S(1)}, bf16[512,512]{1,0:T(8,128)(2,1)S(1)}, u32[]{:S(2)}, u32[]{:S(2)}) collective-permute-start(bf16[512,512]{1,0:T(8,128)(2,1)S(1)} %collective-permute-done.refs_6_), channel_id=1, source_target_pairs={{0,1},{1,0},{2,3},{3,2},{4,5},{5,4},{6,7},{7,6},{8,9},{9,8},{10,11... | collective-permute-start | bytes 1572872 | tf_op jit(solution)/shard_map/ppermute | solution.py:342
  10.3 12.0 %collective-permute-start.4 = (bf16[512,512]{1,0:T(8,128)(2,1)S(1)}, bf16[512,512]{1,0:T(8,128)(2,1)S(1)}, u32[]{:S(2)}, u32[]{:S(2)}) collective-permute-start(bf16[512,512]{1,0:T(8,128)(2,1)S(1)} %collective-permute-done.refs_6_), channel_id=1, source_target_pairs={{0,4},{1,3},{2,6},{3,1},{4,0},{5,7},{6,2},{7,5},{8,10},{9,13},{10,... | collective-permute-start | bytes 1572872 | tf_op jit(solution)/shard_map/ppermute | solution.py:341
  12.4 9.9 %collective-permute-start.5 = (bf16[256,512]{1,0:T(8,128)(2,1)S(1)}, bf16[256,512]{1,0:T(8,128)(2,1)S(1)}, u32[]{:S(2)}, u32[]{:S(2)}) collective-permute-start(bf16[256,512]{1,0:T(8,128)(2,1)S(1)} %slice_bitcast_fusion), channel_id=1, source_target_pairs={{0,4},{1,3},{2,6},{3,1},{4,0},{5,7},{6,2},{7,5},{8,10},{9,13},{10,... | collective-permute-start | bytes 786440 | tf_op jit(solution)/shard_map/ppermute | solution.py:334
  12.5 9.8 %collective-permute-start.3 = (bf16[256,512]{1,0:T(8,128)(2,1)S(1)}, bf16[256,512]{1,0:T(8,128)(2,1)S(1)}, u32[]{:S(2)}, u32[]{:S(2)}) collective-permute-start(bf16[256,512]{1,0:T(8,128)(2,1)S(1)} %slice.9), channel_id=1, source_target_pairs={{0,8},{1,9},{2,10},{3,11},{4,12},{5,13},{6,14},{7,15},{8,0},{9,1},... | collective-permute-start | bytes 786440 | tf_op jit(solution)/shard_map/ppermute | solution.py:340
  22.3 3.9 %collective-permute-start.8 = (bf16[512,512]{1,0:T(8,128)(2,1)S(1)}, bf16[512,512]{1,0:T(8,128)(2,1)S(1)}, u32[]{:S(2)}, u32[]{:S(2)}) collective-permute-start(bf16[512,512]{1,0:T(8,128)(2,1)S(1)} %collective-permute-done.4.refs_2_), channel_id=1, source_target_pairs={{0,1},{1,0},{2,3},{3,2},{4,5},{5,4},{6,7},{7,6},{8,9},{9,8},{10,11... | collective-permute-start | bytes 1572872 | tf_op jit(solution)/shard_map/ppermute | solution.py:352
  22.3 3.9 %collective-permute-start.6 = (bf16[256,512]{1,0:T(8,128)(2,1)S(1)}, bf16[256,512]{1,0:T(8,128)(2,1)S(1)}, u32[]{:S(2)}, u32[]{:S(2)}) collective-permute-start(bf16[256,512]{1,0:T(8,128)(2,1)S(1)} %collective-permute-done.3.refs_0_), channel_id=1, source_target_pairs={{0,1},{1,0},{2,3},{3,2},{4,5},{5,4},{6,7},{7,6},{8,9},{9,8},{10,11... | collective-permute-start | bytes 786440 | tf_op jit(solution)/shard_map/ppermute | solution.py:351
  22.9 3.4 %collective-permute-start.7 = (bf16[256,512]{1,0:T(8,128)(2,1)S(1)}, bf16[256,512]{1,0:T(8,128)(2,1)S(1)}, u32[]{:S(2)}, u32[]{:S(2)}) collective-permute-start(bf16[256,512]{1,0:T(8,128)(2,1)S(1)} %collective-permute-done.5.refs_1_), channel_id=1, source_target_pairs={{0,1},{1,0},{2,3},{3,2},{4,5},{5,4},{6,7},{7,6},{8,9},{9,8},{10,11... | collective-permute-start | bytes 786440 | tf_op jit(solution)/shard_map/ppermute | solution.py:348
  29.8 10.3 %collective-permute-start.10 = (bf16[128,512]{1,0:T(8,128)(2,1)S(1)}, bf16[128,512]{1,0:T(8,128)(2,1)S(1)}, u32[]{:S(2)}, u32[]{:S(2)}) collective-permute-start(bf16[128,512]{1,0:T(8,128)(2,1)S(1)} %get-tuple-element.35), channel_id=1, source_target_pairs={{0,16},{8,24},{16,0},{24,8},{1,17},{9,25},{17,1},{25,9},{2,18},{10... | collective-permute-start | bytes 393224 | tf_op jit(solution)/shard_map/ppermute | solution.py:360
  31.0 11.7 %collective-permute-start.11 = (bf16[128,512]{1,0:T(8,128)(2,1)S(1)}, bf16[128,512]{1,0:T(8,128)(2,1)S(1)}, u32[]{:S(2)}, u32[]{:S(2)}) collective-permute-start(bf16[128,512]{1,0:T(8,128)(2,1)S(1)} %get-tuple-element.36), channel_id=1, source_target_pairs={{0,8},{8,0},{16,24},{24,16},{1,9},{9,1},{17,25},{25,17},{2,10},{10... | collective-permute-start | bytes 393224 | tf_op jit(solution)/shard_map/ppermute | solution.py:360
  33.1 9.6 %collective-permute-start.9 = (bf16[128,512]{1,0:T(8,128)(2,1)S(1)}, bf16[128,512]{1,0:T(8,128)(2,1)S(1)}, u32[]{:S(2)}, u32[]{:S(2)}) collective-permute-start(bf16[128,512]{1,0:T(8,128)(2,1)S(1)} %get-tuple-element.34), channel_id=1, source_target_pairs={{0,24},{8,16},{16,8},{24,0},{1,25},{9,17},{17,9},{25,1},{2,26},{10... | collective-permute-start | bytes 393224 | tf_op jit(solution)/shard_map/ppermute | solution.py:360

commit v2 on v1

--- a/solution.py
+++ b/solution.py
@@ -347,8 +347,9 @@
     second_bottom, total = barrier((second_bottom, total))
     other_second_bottom = lax.ppermute(second_bottom, axes, to_core)
     add = functools.partial(add_blocks, ops=ops, plan=plan, left=left, right=right)
-    second_top, far, total = barrier((second_top, far, total))
+    second_top, total = barrier((second_top, total))
     other_second_top = lax.ppermute(second_top, axes, to_core)
+    far, total, second_top = barrier((far, total, second_top))
     other_far = lax.ppermute(far, axes, to_core)
     (total,) = add([[second_top, second_bottom], [far]], (4, 6), (), before=total)
     _, *parts = add(

time: 43.2 us -> 43.7 us (1.012)
  the two profiles are of different devices: /device:TPU:0 before, /device:TPU:12 now
where the time goes in v2:
time: 43.7 us; the launch traced here: 43.6 us
  waiting for transfers between devices  19.5 us (45%)
  Pallas kernels  15.1 us (35%)
  starting transfers between devices  8.07 us (18%)
  other arithmetic  0.72 us (2%)
    ppermute x3, waiting for transfers between devices, on_eight(): sent = lax.ppermute(parts[flip], 'op', [(i, i ^ flip) for i in range(ops)])  12.1 us
    pallas_call x1, Pallas kernels, start_sum(): pl.pallas_call(functools.partial(first_kernel, position_of, limit), out_s...  5.97 us
    ppermute x1, waiting for transfers between devices, on_eight(): second_bottom = lax.ppermute(own[cut:], axes, to_second)  5.02 us
    pallas_call x2, Pallas kernels, add_blocks(): pl.pallas_call(functools.partial(next_kernel, [len(block) for block in bl...  4.87 us
    pallas_call x1, Pallas kernels, add_and_load(): pl.pallas_call(functools.partial(second_kernel, pieces, places, skip, oth...  4.3 us
    ppermute x3, starting transfers between devices, on_eight(): sent = lax.ppermute(parts[flip], 'op', [(i, i ^ flip) for i in range(ops)])  3.84 us
    ppermute x1, waiting for transfers between devices, on_eight(): first = lax.ppermute(own, axes, to_first)  2.36 us
    ppermute x1, starting transfers between devices, on_eight(): far = lax.ppermute(first, axes, to_second)  1.49 us
  transfers between devices with their start and end apart: 12, of which 5 were waited for; matrix products, arithmetic and copies ran while one was open for 0% of the time, Pallas kernels for 31%

profile of v2, /device:TPU:12, one launch (start us, length us, event | category | flops | bytes accessed | tf_op | source)
XLA Modules:
  0.0 43.6 jit_solution(3983922433223904353)
XLA Ops:
  0.0 0.5 %collective-permute-start = (bf16[512,512]{1,0:T(8,128)(2,1)}, bf16[512,512]{1,0:T(8,128)(2,1)S(1)}, u32[]{:S(2)}, u32[]{:S(2)}) collective-permute-start(bf16[512,512]{1,0:T(8,128)(2,1)} %bitcast.9), channel_id=1, source_target_pairs={{0,2},{1,5},{2,0},{3,7},{4,6},{5,1},{6,4},{7,3},{8,12},{9,11},{10,... | collective-permute-start | bytes 1572872 | tf_op jit(solution)/shard_map/ppermute | solution.py:333
  0.5 0.5 %collective-permute-start.1 = (bf16[512,512]{1,0:T(8,128)(2,1)}, bf16[512,512]{1,0:T(8,128)(2,1)S(1)}, u32[]{:S(2)}, u32[]{:S(2)}) collective-permute-start(bf16[512,512]{1,0:T(8,128)(2,1)} %bitcast.10), channel_id=1, source_target_pairs={{0,1},{1,0},{2,3},{3,2},{4,5},{5,4},{6,7},{7,6},{8,9},{9,8},{10,11... | collective-permute-start | bytes 1572872 | tf_op jit(solution)/shard_map/ppermute | solution.py:335
  1.0 0.0 copy-start
  1.0 6.0 %shard_map.55 = (f32[512,512]{1,0:T(8,128)S(1)}, s32[15]{0:T(128)S(1)}) custom-call(s32[2,15]{1,0:T(2,128)} %bitcast.17, s32[2,8]{1,0:T(2,128)} %bitcast.18, bf16[15,512,512]{2,1,0:T(8,128)(2,1)} %bitcast.13, bf16[15,512,512]{2,1,0:T(8,128)(2,1)} %bitcast.15, bf16[512,512]{1,0:T(8,128)(2,1)} %bitcast.11), custom_call_target="tpu_custom_call" | custom-call | flops 3221225472 | bytes 6291456 | tf_op jit(solution)/shard_map/pallas_call | solution.py:212
  7.0 2.4 %collective-permute-done.refs_6_ = bf16[512,512]{1,0:T(8,128)(2,1)S(1)} collective-permute-done((bf16[512,512]{1,0:T(8,128)(2,1)}, bf16[512,512]{1,0:T(8,128)(2,1)S(1)}, u32[]{:S(2)}, u32[]{:S(2)}) %collective-permute-start) | collective-permute-done | bytes 524320 | tf_op jit(solution)/shard_map/ppermute | solution.py:333
  9.4 0.0 collective-permute-start.2
  9.4 1.5 %collective-permute-start.3 = (bf16[512,512]{1,0:T(8,128)(2,1)S(1)}, bf16[512,512]{1,0:T(8,128)(2,1)S(1)}, u32[]{:S(2)}, u32[]{:S(2)}) collective-permute-start(bf16[512,512]{1,0:T(8,128)(2,1)S(1)} %collective-permute-done.refs_6_), channel_id=1, source_target_pairs={{0,4},{1,3},{2,6},{3,1},{4,0},{5,7},{6,2},{7,5},{8,10},{9,13},{10,... | collective-permute-start | bytes 1572872 | tf_op jit(solution)/shard_map/ppermute | solution.py:341
  10.9 0.0 copy-done
  10.9 0.6 %collective-permute-start.5 = (bf16[256,512]{1,0:T(8,128)(2,1)S(1)}, bf16[256,512]{1,0:T(8,128)(2,1)S(1)}, u32[]{:S(2)}, u32[]{:S(2)}) collective-permute-start(bf16[256,512]{1,0:T(8,128)(2,1)S(1)} %slice_bitcast_fusion), channel_id=1, source_target_pairs={{0,4},{1,3},{2,6},{3,1},{4,0},{5,7},{6,2},{7,5},{8,10},{9,13},{10,... | collective-permute-start | bytes 786440 | tf_op jit(solution)/shard_map/ppermute | solution.py:334
  11.5 0.5 %collective-permute-start.4 = (bf16[256,512]{1,0:T(8,128)(2,1)S(1)}, bf16[256,512]{1,0:T(8,128)(2,1)S(1)}, u32[]{:S(2)}, u32[]{:S(2)}) collective-permute-start(bf16[256,512]{1,0:T(8,128)(2,1)S(1)} %slice.9), channel_id=1, source_target_pairs={{0,8},{1,9},{2,10},{3,11},{4,12},{5,13},{6,14},{7,15},{8,0},{9,1},... | collective-permute-start | bytes 786440 | tf_op jit(solution)/shard_map/ppermute | solution.py:340
  12.0 0.0 collective-permute-done.1.refs_5_
  12.1 0.0 collective-permute-done.2.refs_7_
  12.1 4.3 %shard_map.56 = (f32[512,512]{1,0:T(8,128)S(1)}, bf16[15,512,512]{2,1,0:T(8,128)(2,1)S(1)}, bf16[15,512,512]{2,1,0:T(8,128)(2,1)S(1)}) custom-call(s32[15]{0:T(128)S(1)} %get-tuple-element.23.refs_0_.plan, bf16[15,512,512]{2,1,0:T(8,128)(2,1)} %bitcast.14, bf16[15,512,512]{2,1,0:T(8,128)(2,1)} %bitcast.16, ...), custom_call_target="tpu_custom_call", output_to_operand_aliasing={{0}: (3, {})} | custom-call | flops 4026531840 | bytes 15728640 | tf_op jit(solution)/shard_map/pallas_call | solution.py:241
  16.4 5.0 %collective-permute-done.5.refs_1_ = bf16[256,512]{1,0:T(8,128)(2,1)S(1)} collective-permute-done((bf16[256,512]{1,0:T(8,128)(2,1)S(1)}, bf16[256,512]{1,0:T(8,128)(2,1)S(1)}, u32[]{:S(2)}, u32[]{:S(2)}) %collective-permute-start.5) | collective-permute-done | bytes 262176 | tf_op jit(solution)/shard_map/ppermute | solution.py:334
  21.4 0.0 collective-permute-done.4.refs_0_
  21.4 0.0 collective-permute-done.3.refs_2_
  21.4 0.0 collective-permute-start.8
  21.4 0.5 %collective-permute-start.6 = (bf16[256,512]{1,0:T(8,128)(2,1)S(1)}, bf16[256,512]{1,0:T(8,128)(2,1)S(1)}, u32[]{:S(2)}, u32[]{:S(2)}) collective-permute-start(bf16[256,512]{1,0:T(8,128)(2,1)S(1)} %collective-permute-done.4.refs_0_), channel_id=1, source_target_pairs={{0,1},{1,0},{2,3},{3,2},{4,5},{5,4},{6,7},{7,6},{8,9},{9,8},{10,11... | collective-permute-start | bytes 786440 | tf_op jit(solution)/shard_map/ppermute | solution.py:351
  21.9 0.1 collective-permute-start.7
  22.0 3.3 %shard_map.57.before = f32[512,512]{1,0:T(8,128)S(1)} custom-call(s32[15]{0:T(128)S(1)} %get-tuple-element.23.refs_0_.plan, bf16[15,512,512]{2,1,0:T(8,128)(2,1)S(1)} %get-tuple-element.27.left, bf16[15,512,512]{2,1,0:T(8,128)(2,1)S(1)} %get-tuple-element.28.right, f32[512,512]{1,0:T(8,128)S(1)} %get-tuple-element.33.before, ...), custom_call_target="tpu_custom_call", output_to_operand_aliasing={{}: (3, {})} | custom-call | flops 2013265920 | bytes 3932160 | tf_op jit(solution)/shard_map/pallas_call | solution.py:267
  25.3 0.0 collective-permute-done.6.refs_0_
  25.3 0.0 collective-permute-done.7.refs_1_
  25.3 0.0 collective-permute-done.8.refs_2_
  25.3 1.6 %shard_map.58 = (f32[512,512]{1,0:T(8,128)S(1)}, f32[128,512]{1,0:T(8,128)S(1)}, bf16[128,512]{1,0:T(8,128)(2,1)S(1)}, bf16[128,512]{1,0:T(8,128)(2,1)S(1)}, bf16[128,512]{1,0:T(8,128)(2,1)S(1)}) custom-call(s32[15]{0:T(128)S(1)} %get-tuple-element.23.refs_0_.plan, ...), custom_call_target="tpu_custom_call", output_to_operand_aliasing={{0}: (3, {})} | custom-call | flops 2013265920 | bytes 3932160 | tf_op jit(solution)/shard_map/pallas_call | solution.py:267
  26.9 3.2 %collective-permute-start.10 = (bf16[128,512]{1,0:T(8,128)(2,1)S(1)}, bf16[128,512]{1,0:T(8,128)(2,1)S(1)}, u32[]{:S(2)}, u32[]{:S(2)}) collective-permute-start(bf16[128,512]{1,0:T(8,128)(2,1)S(1)} %get-tuple-element.39), channel_id=1, source_target_pairs={{0,16},{8,24},{16,0},{24,8},{1,17},{9,25},{17,1},{25,9},{2,18},{10... | collective-permute-start | bytes 393224 | tf_op jit(solution)/shard_map/ppermute | solution.py:361
  30.1 0.0 collective-permute-start.11
  30.1 0.6 %collective-permute-start.9 = (bf16[128,512]{1,0:T(8,128)(2,1)S(1)}, bf16[128,512]{1,0:T(8,128)(2,1)S(1)}, u32[]{:S(2)}, u32[]{:S(2)}) collective-permute-start(bf16[128,512]{1,0:T(8,128)(2,1)S(1)} %get-tuple-element.38), channel_id=1, source_target_pairs={{0,24},{8,16},{16,8},{24,0},{1,25},{9,17},{17,9},{25,1},{2,26},{10... | collective-permute-start | bytes 393224 | tf_op jit(solution)/shard_map/ppermute | solution.py:361
  30.7 4.6 %collective-permute-done.10 = bf16[128,512]{1,0:T(8,128)(2,1)S(1)} collective-permute-done((bf16[128,512]{1,0:T(8,128)(2,1)S(1)}, bf16[128,512]{1,0:T(8,128)(2,1)S(1)}, u32[]{:S(2)}, u32[]{:S(2)}) %collective-permute-start.10) | collective-permute-done | bytes 131104 | tf_op jit(solution)/shard_map/ppermute | solution.py:361
  35.4 1.0 %collective-permute-done.11 = bf16[128,512]{1,0:T(8,128)(2,1)S(1)} collective-permute-done((bf16[128,512]{1,0:T(8,128)(2,1)S(1)}, bf16[128,512]{1,0:T(8,128)(2,1)S(1)}, u32[]{:S(2)}, u32[]{:S(2)}) %collective-permute-start.11) | collective-permute-done | bytes 131104 | tf_op jit(solution)/shard_map/ppermute | solution.py:361
  36.4 6.4 %collective-permute-done.9 = bf16[128,512]{1,0:T(8,128)(2,1)S(1)} collective-permute-done((bf16[128,512]{1,0:T(8,128)(2,1)S(1)}, bf16[128,512]{1,0:T(8,128)(2,1)S(1)}, u32[]{:S(2)}, u32[]{:S(2)}) %collective-permute-start.9) | collective-permute-done | bytes 131104 | tf_op jit(solution)/shard_map/ppermute | solution.py:361
  42.9 0.7 %fusion = bf16[128,1,512]{2,0,1:T(8,128)(2,1)} fusion(bf16[128,512]{1,0:T(8,128)(2,1)S(1)} %collective-permute-done.11, bf16[128,512]{1,0:T(8,128)(2,1)S(1)} %collective-permute-done.10, f32[128,512]{1,0:T(8,128)S(1)} %get-tuple-element.37, bf16[128,512]{1,0:T(8,128)(2,1)S(1)} %collective-permute-done.9), kind=kLoop, calls=%fused_computation.2 | loop fusion | flops 458752 | bytes 786432 | tf_op jit(solution)/shard_map/broadcast_in_dim | solution.py:390
  (2 shorter events, 0.0 us)
Async XLA Ops:
  0.0 9.4 %collective-permute-start = (bf16[512,512]{1,0:T(8,128)(2,1)}, bf16[512,512]{1,0:T(8,128)(2,1)S(1)}, u32[]{:S(2)}, u32[]{:S(2)}) collective-permute-start(bf16[512,512]{1,0:T(8,128)(2,1)} %bitcast.9), channel_id=1, source_target_pairs={{0,2},{1,5},{2,0},{3,7},{4,6},{5,1},{6,4},{7,3},{8,12},{9,11},{10,... | collective-permute-start | bytes 1572872 | tf_op jit(solution)/shard_map/ppermute | solution.py:333
  0.5 11.5 %collective-permute-start.1 = (bf16[512,512]{1,0:T(8,128)(2,1)}, bf16[512,512]{1,0:T(8,128)(2,1)S(1)}, u32[]{:S(2)}, u32[]{:S(2)}) collective-permute-start(bf16[512,512]{1,0:T(8,128)(2,1)} %bitcast.10), channel_id=1, source_target_pairs={{0,1},{1,0},{2,3},{3,2},{4,5},{5,4},{6,7},{7,6},{8,9},{9,8},{10,11... | collective-permute-start | bytes 1572872 | tf_op jit(solution)/shard_map/ppermute | solution.py:335
  1.0 9.8 %copy-start = (bf16[512,1,512]{2,0,1:T(8,128)(2,1)S(1)}, bf16[512,1,512]{2,0,1:T(8,128)(2,1)}, u32[]{:S(2)}) copy-start(bf16[512,1,512]{2,0,1:T(8,128)(2,1)} %param.5) | copy-start | bytes 1572868
  9.4 2.7 %collective-permute-start.2 = (bf16[512,512]{1,0:T(8,128)(2,1)S(1)}, bf16[512,512]{1,0:T(8,128)(2,1)S(1)}, u32[]{:S(2)}, u32[]{:S(2)}) collective-permute-start(bf16[512,512]{1,0:T(8,128)(2,1)S(1)} %collective-permute-done.refs_6_), channel_id=1, source_target_pairs={{0,1},{1,0},{2,3},{3,2},{4,5},{5,4},{6,7},{7,6},{8,9},{9,8},{10,11... | collective-permute-start | bytes 1572872 | tf_op jit(solution)/shard_map/ppermute | solution.py:342
  9.4 12.0 %collective-permute-start.3 = (bf16[512,512]{1,0:T(8,128)(2,1)S(1)}, bf16[512,512]{1,0:T(8,128)(2,1)S(1)}, u32[]{:S(2)}, u32[]{:S(2)}) collective-permute-start(bf16[512,512]{1,0:T(8,128)(2,1)S(1)} %collective-permute-done.refs_6_), channel_id=1, source_target_pairs={{0,4},{1,3},{2,6},{3,1},{4,0},{5,7},{6,2},{7,5},{8,10},{9,13},{10,... | collective-permute-start | bytes 1572872 | tf_op jit(solution)/shard_map/ppermute | solution.py:341
  10.9 10.5 %collective-permute-start.5 = (bf16[256,512]{1,0:T(8,128)(2,1)S(1)}, bf16[256,512]{1,0:T(8,128)(2,1)S(1)}, u32[]{:S(2)}, u32[]{:S(2)}) collective-permute-start(bf16[256,512]{1,0:T(8,128)(2,1)S(1)} %slice_bitcast_fusion), channel_id=1, source_target_pairs={{0,4},{1,3},{2,6},{3,1},{4,0},{5,7},{6,2},{7,5},{8,10},{9,13},{10,... | collective-permute-start | bytes 786440 | tf_op jit(solution)/shard_map/ppermute | solution.py:334
  11.5 9.9 %collective-permute-start.4 = (bf16[256,512]{1,0:T(8,128)(2,1)S(1)}, bf16[256,512]{1,0:T(8,128)(2,1)S(1)}, u32[]{:S(2)}, u32[]{:S(2)}) collective-permute-start(bf16[256,512]{1,0:T(8,128)(2,1)S(1)} %slice.9), channel_id=1, source_target_pairs={{0,8},{1,9},{2,10},{3,11},{4,12},{5,13},{6,14},{7,15},{8,0},{9,1},... | collective-permute-start | bytes 786440 | tf_op jit(solution)/shard_map/ppermute | solution.py:340
  21.4 3.9 %collective-permute-start.8 = (bf16[512,512]{1,0:T(8,128)(2,1)S(1)}, bf16[512,512]{1,0:T(8,128)(2,1)S(1)}, u32[]{:S(2)}, u32[]{:S(2)}) collective-permute-start(bf16[512,512]{1,0:T(8,128)(2,1)S(1)} %collective-permute-done.3.refs_2_), channel_id=1, source_target_pairs={{0,1},{1,0},{2,3},{3,2},{4,5},{5,4},{6,7},{7,6},{8,9},{9,8},{10,11... | collective-permute-start | bytes 1572872 | tf_op jit(solution)/shard_map/ppermute | solution.py:353
  21.4 3.9 %collective-permute-start.6 = (bf16[256,512]{1,0:T(8,128)(2,1)S(1)}, bf16[256,512]{1,0:T(8,128)(2,1)S(1)}, u32[]{:S(2)}, u32[]{:S(2)}) collective-permute-start(bf16[256,512]{1,0:T(8,128)(2,1)S(1)} %collective-permute-done.4.refs_0_), channel_id=1, source_target_pairs={{0,1},{1,0},{2,3},{3,2},{4,5},{5,4},{6,7},{7,6},{8,9},{9,8},{10,11... | collective-permute-start | bytes 786440 | tf_op jit(solution)/shard_map/ppermute | solution.py:351
  21.9 3.4 %collective-permute-start.7 = (bf16[256,512]{1,0:T(8,128)(2,1)S(1)}, bf16[256,512]{1,0:T(8,128)(2,1)S(1)}, u32[]{:S(2)}, u32[]{:S(2)}) collective-permute-start(bf16[256,512]{1,0:T(8,128)(2,1)S(1)} %collective-permute-done.5.refs_1_), channel_id=1, source_target_pairs={{0,1},{1,0},{2,3},{3,2},{4,5},{5,4},{6,7},{7,6},{8,9},{9,8},{10,11... | collective-permute-start | bytes 786440 | tf_op jit(solution)/shard_map/ppermute | solution.py:348
  26.9 8.5 %collective-permute-start.10 = (bf16[128,512]{1,0:T(8,128)(2,1)S(1)}, bf16[128,512]{1,0:T(8,128)(2,1)S(1)}, u32[]{:S(2)}, u32[]{:S(2)}) collective-permute-start(bf16[128,512]{1,0:T(8,128)(2,1)S(1)} %get-tuple-element.39), channel_id=1, source_target_pairs={{0,16},{8,24},{16,0},{24,8},{1,17},{9,25},{17,1},{25,9},{2,18},{10... | collective-permute-start | bytes 393224 | tf_op jit(solution)/shard_map/ppermute | solution.py:361
  30.1 6.3 %collective-permute-start.11 = (bf16[128,512]{1,0:T(8,128)(2,1)S(1)}, bf16[128,512]{1,0:T(8,128)(2,1)S(1)}, u32[]{:S(2)}, u32[]{:S(2)}) collective-permute-start(bf16[128,512]{1,0:T(8,128)(2,1)S(1)} %get-tuple-element.40), channel_id=1, source_target_pairs={{0,8},{8,0},{16,24},{24,16},{1,9},{9,1},{17,25},{25,17},{2,10},{10... | collective-permute-start | bytes 393224 | tf_op jit(solution)/shard_map/ppermute | solution.py:361
  30.1 12.8 %collective-permute-start.9 = (bf16[128,512]{1,0:T(8,128)(2,1)S(1)}, bf16[128,512]{1,0:T(8,128)(2,1)S(1)}, u32[]{:S(2)}, u32[]{:S(2)}) collective-permute-start(bf16[128,512]{1,0:T(8,128)(2,1)S(1)} %get-tuple-element.38), channel_id=1, source_target_pairs={{0,24},{8,16},{16,8},{24,0},{1,25},{9,17},{17,9},{25,1},{2,26},{10... | collective-permute-start | bytes 393224 | tf_op jit(solution)/shard_map/ppermute | solution.py:361

commit v3 on v2

--- a/solution.py
+++ b/solution.py
@@ -58,11 +58,25 @@
     return lax.dot_general(halfway, right[...], (((1,), (1,)), ((), ())), preferred_element_type=jnp.float32)
 
 
-def add_operators(total, count, order, left, right, source, ready):
+def sort_operators(plan, orders):
+    for place in range(orders.shape[0]):
+        orders[place, 0] = 0
+
+    def visit(b, carry):
+        place = jnp.maximum(plan[b], 0)
+        count = orders[place, 0] + 1
+        orders[place, count] = b
+        orders[place, 0] = jnp.where(plan[b] < 0, count - 1, count)
+        return carry
+
+    lax.fori_loop(0, plan.shape[0], visit, 0)
+
+
+def add_operators(total, count, pick, left, right, ready):
     def term(i):
-        b = order[0, i]
+        b, source = pick(i)
         ready(b)
-        return left.at[b], source(order[1, i]), right.at[b]
+        return left.at[b], source, right.at[b]
 
     def pair(i, carry):
         one, two = term(2 * i), term(2 * i + 1)
@@ -136,14 +150,13 @@
 
     def start(i, carry):
         loads.start(order[0, i], i)
-        order[0, i] = i
         return carry
 
     lax.fori_loop(0, count, start, 0)
     total[...] = jnp.zeros_like(total)
     copies[2].wait()
     add_operators(
-        total, count, order, left, right, lambda at: [source.at[at]], lambda at: loads.wait(0, at)
+        total, count, lambda i: (i, [source.at[0]]), left, right, lambda at: loads.wait(0, at)
     )
 
 
@@ -151,29 +164,32 @@
     plan, left_hbm, right_hbm = refs[:3]
     n_in = sum(len(p) for p in pieces)
     inputs, rest = refs[4 : 4 + n_in], refs[4 + n_in :]
-    total, left, right, source, now, later, sems, source_sems = rest
+    total, orders, left, right, source, now, later, sems, source_sems = rest
     loads = Loads(left_hbm, right_hbm, left, right, sems)
     sources = load_sources(pieces, inputs, source, source_sems)
     count = list_operators(plan, now, places, skip)
     each(count, now, loads.start)
     behind = list_operators(plan, later, others)
     each(behind, later, loads.start)
+    sort_operators(plan, orders)
     for copy in sources:
         copy.wait()
-    add_operators(total, count, now, left, right, lambda at: [source.at[at]], loads.wait)
+    add_operators(
+        total, count, lambda i: (now[0, i], [source.at[now[1, i]]]), left, right, loads.wait
+    )
     each(behind, later, loads.wait)
 
 
-def next_kernel(counts, places, sends, plan, left, right, before, *refs):
+def next_kernel(counts, places, sends, orders, left, right, before, *refs):
     del before
-    flat = refs[: sum(counts)]
-    total, *outs, order = refs[sum(counts) :]
+    flat, (total, *outs) = refs[: sum(counts)], refs[sum(counts) :]
     begin = 0
     for n, place in zip(counts, places):
         block = flat[begin : begin + n]
         begin += n
-        count = list_operators(plan, order, [place])
-        add_operators(total, count, order, left, right, lambda at: block, lambda b: None)
+        add_operators(
+            total, orders[place, 0], lambda i: (orders[place, i + 1], block), left, right, lambda b: None
+        )
     for out, flip in zip(outs, sends):
         rows = out.shape[0]
         at = pl.multiple_of((lax.axis_index("op") ^ flip) * rows, rows)
@@ -191,7 +207,9 @@
     each(count, order, loads.start)
     total[...] = jnp.zeros_like(total)
     copy.wait()
-    add_operators(total, count, order, left, right, lambda at: [source.at[at]], loads.wait)
+    add_operators(
+        total, count, lambda i: (order[0, i], [source.at[order[1, i]]]), left, right, loads.wait
+    )
 
 
 def cost(flops, moved):
@@ -242,11 +260,12 @@
         functools.partial(second_kernel, pieces, places, skip, others),
         out_shape=[
             jax.ShapeDtypeStruct(before.shape, jnp.float32),
+            jax.ShapeDtypeStruct((8, operators + 2), jnp.int32),
             jax.ShapeDtypeStruct(left_env.shape, left_env.dtype),
             jax.ShapeDtypeStruct(right_env.shape, right_env.dtype),
         ],
         in_specs=[SMEM, HBM, HBM, VMEM] + [ANY] * len(flat),
-        out_specs=[VMEM] * 3,
+        out_specs=[VMEM, SMEM, VMEM, VMEM],
         input_output_aliases={3: 0},
         scratch_shapes=[
             pltpu.VMEM((len(blocks), inner, width), jnp.bfloat16),
@@ -260,7 +279,7 @@
     )(plan, in_hbm(left_env), in_hbm(right_env), before, *flat)
 
 
-def add_blocks(blocks, places, sends, ops, plan, left, right, before):
+def add_blocks(blocks, places, sends, ops, orders, left, right, before):
     flat = [p for block in blocks for p in block]
     operators, rows, inner = left.shape
     columns, width = right.shape[1:]
@@ -273,11 +292,10 @@
         ],
         in_specs=[SMEM] + [VMEM] * (3 + len(flat)),
         out_specs=[VMEM] * (1 + len(sends)),
-        scratch_shapes=[pltpu.SMEM((2, operators + 1), jnp.int32)],
         input_output_aliases={3: 0},
         compiler_params=limit_vmem(16),
         cost_estimate=cost(operators * rows * inner * width, operators * rows * inner),
-    )(plan, left, right, before, *flat)
+    )(orders, left, right, before, *flat)
 
 
 def sum_all(blocks, shift, charge, left_env, right_env):
@@ -340,13 +358,13 @@
     second_top = lax.ppermute(first[:cut], axes, to_plane)
     far = lax.ppermute(first, axes, to_second)
     other_first = lax.ppermute(first, axes, to_core)
-    total, left, right = add_and_load(
+    total, orders, left, right = add_and_load(
         [[own], [other], [first], [other_first]], (0, 1, 2, 5), LIMIT, later,
         plan, left_env, right_env, total,
     )
     second_bottom, total = barrier((second_bottom, total))
     other_second_bottom = lax.ppermute(second_bottom, axes, to_core)
-    add = functools.partial(add_blocks, ops=ops, plan=plan, left=left, right=right)
+    add = functools.partial(add_blocks, ops=ops, orders=orders, left=left, right=right)
     second_top, total = barrier((second_top, total))
     other_second_top = lax.ppermute(second_top, axes, to_core)
     far, total, second_top = barrier((far, total, second_top))

time: 43.7 us -> 42.1 us (0.963)
  the two profiles are of different devices: /device:TPU:12 before, /device:TPU:17 now
where the time goes in v3:
time: 42.1 us; the launch traced here: 41.8 us
  Pallas kernels  16 us (38%)
  waiting for transfers between devices  12.8 us (30%)
  starting transfers between devices  12.2 us (29%)
  other arithmetic  0.72 us (2%)
    ppermute x3, waiting for transfers between devices, on_eight(): sent = lax.ppermute(parts[flip], 'op', [(i, i ^ flip) for i in range(ops)])  10.1 us
    pallas_call x1, Pallas kernels, start_sum(): pl.pallas_call(functools.partial(first_kernel, position_of, limit), out_s...  6.75 us
    pallas_call x1, Pallas kernels, add_and_load(): pl.pallas_call(functools.partial(second_kernel, pieces, places, skip, oth...  6.66 us
    ppermute x3, starting transfers between devices, on_eight(): sent = lax.ppermute(parts[flip], 'op', [(i, i ^ flip) for i in range(ops)])  4.66 us
    pallas_call x2, Pallas kernels, add_blocks(): pl.pallas_call(functools.partial(next_kernel, [len(block) for block in bl...  2.59 us
    ppermute x1, waiting for transfers between devices, on_eight(): second_bottom = lax.ppermute(own[cut:], axes, to_second)  1.52 us
    ppermute x1, starting transfers between devices, on_eight(): second_top = lax.ppermute(first[:cut], axes, to_plane)  1.36 us
    ppermute x1, starting transfers between devices, on_eight(): first = lax.ppermute(own, axes, to_first)  1.24 us
  transfers between devices with their start and end apart: 12, of which 6 were waited for; matrix products, arithmetic and copies ran while one was open for 0% of the time, Pallas kernels for 34%

profile of v3, /device:TPU:17, one launch (start us, length us, event | category | flops | bytes accessed | tf_op | source)
XLA Modules:
  0.0 41.8 jit_solution(16031058515131089147)
XLA Ops:
  0.0 1.2 %collective-permute-start = (bf16[512,512]{1,0:T(8,128)(2,1)}, bf16[512,512]{1,0:T(8,128)(2,1)S(1)}, u32[]{:S(2)}, u32[]{:S(2)}) collective-permute-start(bf16[512,512]{1,0:T(8,128)(2,1)} %bitcast.9), channel_id=1, source_target_pairs={{0,2},{1,5},{2,0},{3,7},{4,6},{5,1},{6,4},{7,3},{8,12},{9,11},{10,... | collective-permute-start | bytes 1572872 | tf_op jit(solution)/shard_map/ppermute | solution.py:351
  1.2 0.9 %collective-permute-start.1 = (bf16[512,512]{1,0:T(8,128)(2,1)}, bf16[512,512]{1,0:T(8,128)(2,1)S(1)}, u32[]{:S(2)}, u32[]{:S(2)}) collective-permute-start(bf16[512,512]{1,0:T(8,128)(2,1)} %bitcast.10), channel_id=1, source_target_pairs={{0,1},{1,0},{2,3},{3,2},{4,5},{5,4},{6,7},{7,6},{8,9},{9,8},{10,11... | collective-permute-start | bytes 1572872 | tf_op jit(solution)/shard_map/ppermute | solution.py:353
  2.2 0.0 copy-start
  2.2 6.7 %shard_map.55 = (f32[512,512]{1,0:T(8,128)S(1)}, s32[15]{0:T(128)S(1)}) custom-call(s32[2,15]{1,0:T(2,128)} %bitcast.17, s32[2,8]{1,0:T(2,128)} %bitcast.18, bf16[15,512,512]{2,1,0:T(8,128)(2,1)} %bitcast.13, bf16[15,512,512]{2,1,0:T(8,128)(2,1)} %bitcast.15, bf16[512,512]{1,0:T(8,128)(2,1)} %bitcast.11), custom_call_target="tpu_custom_call" | custom-call | flops 3221225472 | bytes 6291456 | tf_op jit(solution)/shard_map/pallas_call | solution.py:230
  8.9 0.0 collective-permute-done.refs_6_
  8.9 1.1 %collective-permute-start.2 = (bf16[512,512]{1,0:T(8,128)(2,1)S(1)}, bf16[512,512]{1,0:T(8,128)(2,1)S(1)}, u32[]{:S(2)}, u32[]{:S(2)}) collective-permute-start(bf16[512,512]{1,0:T(8,128)(2,1)S(1)} %collective-permute-done.refs_6_), channel_id=1, source_target_pairs={{0,1},{1,0},{2,3},{3,2},{4,5},{5,4},{6,7},{7,6},{8,9},{9,8},{10,11... | collective-permute-start | bytes 1572872 | tf_op jit(solution)/shard_map/ppermute | solution.py:360
  10.1 1.2 %collective-permute-start.3 = (bf16[512,512]{1,0:T(8,128)(2,1)S(1)}, bf16[512,512]{1,0:T(8,128)(2,1)S(1)}, u32[]{:S(2)}, u32[]{:S(2)}) collective-permute-start(bf16[512,512]{1,0:T(8,128)(2,1)S(1)} %collective-permute-done.refs_6_), channel_id=1, source_target_pairs={{0,4},{1,3},{2,6},{3,1},{4,0},{5,7},{6,2},{7,5},{8,10},{9,13},{10,... | collective-permute-start | bytes 1572872 | tf_op jit(solution)/shard_map/ppermute | solution.py:359
  11.3 0.0 copy-done
  11.3 0.3 collective-permute-start.5
  11.6 1.4 %collective-permute-start.4 = (bf16[256,512]{1,0:T(8,128)(2,1)S(1)}, bf16[256,512]{1,0:T(8,128)(2,1)S(1)}, u32[]{:S(2)}, u32[]{:S(2)}) collective-permute-start(bf16[256,512]{1,0:T(8,128)(2,1)S(1)} %slice.9), channel_id=1, source_target_pairs={{0,8},{1,9},{2,10},{3,11},{4,12},{5,13},{6,14},{7,15},{8,0},{9,1},... | collective-permute-start | bytes 786440 | tf_op jit(solution)/shard_map/ppermute | solution.py:358
  13.0 0.0 collective-permute-done.1.refs_5_
  13.0 0.0 collective-permute-done.2.refs_7_
  13.0 6.7 %shard_map.56 = (f32[512,512]{1,0:T(8,128)S(1)}, s32[8,17]{1,0:T(8,128)S(1)}, bf16[15,512,512]{2,1,0:T(8,128)(2,1)S(1)}, bf16[15,512,512]{2,1,0:T(8,128)(2,1)S(1)}) custom-call(s32[15]{0:T(128)S(1)} %get-tuple-element.24.refs_0_, bf16[15,512,512]{2,1,0:T(8,128)(2,1)} %bitcast.14, bf16[15,512,512]{2,1,0:T(8,128)(2,1)} %bitcast.16, ...), custom_call_target="tpu_custom_call", output_to_operand_aliasing={{0}: (3, {})} | custom-call | flops 4026531840 | bytes 15728640 | tf_op jit(solution)/shard_map/pallas_call | solution.py:259
  19.7 1.5 %collective-permute-done.5.refs_1_ = bf16[256,512]{1,0:T(8,128)(2,1)S(1)} collective-permute-done((bf16[256,512]{1,0:T(8,128)(2,1)S(1)}, bf16[256,512]{1,0:T(8,128)(2,1)S(1)}, u32[]{:S(2)}, u32[]{:S(2)}) %collective-permute-start.5) | collective-permute-done | bytes 262176 | tf_op jit(solution)/shard_map/ppermute | solution.py:352
  21.2 0.0 collective-permute-done.4.refs_0_
  21.2 0.0 collective-permute-done.3.refs_2_
  21.2 0.9 %collective-permute-start.8 = (bf16[512,512]{1,0:T(8,128)(2,1)S(1)}, bf16[512,512]{1,0:T(8,128)(2,1)S(1)}, u32[]{:S(2)}, u32[]{:S(2)}) collective-permute-start(bf16[512,512]{1,0:T(8,128)(2,1)S(1)} %collective-permute-done.3.refs_2_), channel_id=1, source_target_pairs={{0,1},{1,0},{2,3},{3,2},{4,5},{5,4},{6,7},{7,6},{8,9},{9,8},{10,11... | collective-permute-start | bytes 1572872 | tf_op jit(solution)/shard_map/ppermute | solution.py:371
  22.1 0.1 collective-permute-start.6
  22.1 0.4 %collective-permute-start.7 = (bf16[256,512]{1,0:T(8,128)(2,1)S(1)}, bf16[256,512]{1,0:T(8,128)(2,1)S(1)}, u32[]{:S(2)}, u32[]{:S(2)}) collective-permute-start(bf16[256,512]{1,0:T(8,128)(2,1)S(1)} %collective-permute-done.5.refs_1_), channel_id=1, source_target_pairs={{0,1},{1,0},{2,3},{3,2},{4,5},{5,4},{6,7},{7,6},{8,9},{9,8},{10,11... | collective-permute-start | bytes 786440 | tf_op jit(solution)/shard_map/ppermute | solution.py:366
  22.6 0.6 %shard_map.57.before = f32[512,512]{1,0:T(8,128)S(1)} custom-call(s32[8,17]{1,0:T(8,128)S(1)} %get-tuple-element.28.orders, bf16[15,512,512]{2,1,0:T(8,128)(2,1)S(1)} %get-tuple-element.29.left, bf16[15,512,512]{2,1,0:T(8,128)(2,1)S(1)} %get-tuple-element.30.right, f32[512,512]{1,0:T(8,128)S(1)} %get-tuple-element.35.before, ...), custom_call_target="tpu_custom_call", output_to_operand_aliasing={{}: (3, {})} | custom-call | flops 2013265920 | bytes 3932160 | tf_op jit(solution)/shard_map/pallas_call | solution.py:286
  23.2 0.8 %collective-permute-done.6.refs_0_ = bf16[256,512]{1,0:T(8,128)(2,1)S(1)} collective-permute-done((bf16[256,512]{1,0:T(8,128)(2,1)S(1)}, bf16[256,512]{1,0:T(8,128)(2,1)S(1)}, u32[]{:S(2)}, u32[]{:S(2)}) %collective-permute-start.6) | collective-permute-done | bytes 262176 | tf_op jit(solution)/shard_map/ppermute | solution.py:369
  24.0 0.4 collective-permute-done.7.refs_1_
  24.4 0.0 collective-permute-done.8.refs_2_
  24.4 2.0 %shard_map.58 = (f32[512,512]{1,0:T(8,128)S(1)}, f32[128,512]{1,0:T(8,128)S(1)}, bf16[128,512]{1,0:T(8,128)(2,1)S(1)}, bf16[128,512]{1,0:T(8,128)(2,1)S(1)}, bf16[128,512]{1,0:T(8,128)(2,1)S(1)}) custom-call(s32[8,17]{1,0:T(8,128)S(1)} %get-tuple-element.28.orders, ...), custom_call_target="tpu_custom_call", output_to_operand_aliasing={{0}: (3, {})} | custom-call | flops 2013265920 | bytes 3932160 | tf_op jit(solution)/shard_map/pallas_call | solution.py:286
  26.3 0.3 collective-permute-start.10
  26.6 3.2 %collective-permute-start.11 = (bf16[128,512]{1,0:T(8,128)(2,1)S(1)}, bf16[128,512]{1,0:T(8,128)(2,1)S(1)}, u32[]{:S(2)}, u32[]{:S(2)}) collective-permute-start(bf16[128,512]{1,0:T(8,128)(2,1)S(1)} %get-tuple-element.42), channel_id=1, source_target_pairs={{0,8},{8,0},{16,24},{24,16},{1,9},{9,1},{17,25},{25,17},{2,10},{10... | collective-permute-start | bytes 393224 | tf_op jit(solution)/shard_map/ppermute | solution.py:379
  29.9 1.1 %collective-permute-start.9 = (bf16[128,512]{1,0:T(8,128)(2,1)S(1)}, bf16[128,512]{1,0:T(8,128)(2,1)S(1)}, u32[]{:S(2)}, u32[]{:S(2)}) collective-permute-start(bf16[128,512]{1,0:T(8,128)(2,1)S(1)} %get-tuple-element.40), channel_id=1, source_target_pairs={{0,24},{8,16},{16,8},{24,0},{1,25},{9,17},{17,9},{25,1},{2,26},{10... | collective-permute-start | bytes 393224 | tf_op jit(solution)/shard_map/ppermute | solution.py:379
  31.0 0.2 collective-permute-done.10
  31.2 5.5 %collective-permute-done.11 = bf16[128,512]{1,0:T(8,128)(2,1)S(1)} collective-permute-done((bf16[128,512]{1,0:T(8,128)(2,1)S(1)}, bf16[128,512]{1,0:T(8,128)(2,1)S(1)}, u32[]{:S(2)}, u32[]{:S(2)}) %collective-permute-start.11) | collective-permute-done | bytes 131104 | tf_op jit(solution)/shard_map/ppermute | solution.py:379
  36.6 4.4 %collective-permute-done.9 = bf16[128,512]{1,0:T(8,128)(2,1)S(1)} collective-permute-done((bf16[128,512]{1,0:T(8,128)(2,1)S(1)}, bf16[128,512]{1,0:T(8,128)(2,1)S(1)}, u32[]{:S(2)}, u32[]{:S(2)}) %collective-permute-start.9) | collective-permute-done | bytes 131104 | tf_op jit(solution)/shard_map/ppermute | solution.py:379
  41.1 0.7 %fusion = bf16[128,1,512]{2,0,1:T(8,128)(2,1)} fusion(bf16[128,512]{1,0:T(8,128)(2,1)S(1)} %collective-permute-done.11, bf16[128,512]{1,0:T(8,128)(2,1)S(1)} %collective-permute-done.10, f32[128,512]{1,0:T(8,128)S(1)} %get-tuple-element.39, bf16[128,512]{1,0:T(8,128)(2,1)S(1)} %collective-permute-done.9), kind=kLoop, calls=%fused_computation.2 | loop fusion | flops 458752 | bytes 786432 | tf_op jit(solution)/shard_map/broadcast_in_dim | solution.py:408
  (2 shorter events, 0.0 us)
Async XLA Ops:
  0.0 8.9 %collective-permute-start = (bf16[512,512]{1,0:T(8,128)(2,1)}, bf16[512,512]{1,0:T(8,128)(2,1)S(1)}, u32[]{:S(2)}, u32[]{:S(2)}) collective-permute-start(bf16[512,512]{1,0:T(8,128)(2,1)} %bitcast.9), channel_id=1, source_target_pairs={{0,2},{1,5},{2,0},{3,7},{4,6},{5,1},{6,4},{7,3},{8,12},{9,11},{10,... | collective-permute-start | bytes 1572872 | tf_op jit(solution)/shard_map/ppermute | solution.py:351
  1.2 11.8 %collective-permute-start.1 = (bf16[512,512]{1,0:T(8,128)(2,1)}, bf16[512,512]{1,0:T(8,128)(2,1)S(1)}, u32[]{:S(2)}, u32[]{:S(2)}) collective-permute-start(bf16[512,512]{1,0:T(8,128)(2,1)} %bitcast.10), channel_id=1, source_target_pairs={{0,1},{1,0},{2,3},{3,2},{4,5},{5,4},{6,7},{7,6},{8,9},{9,8},{10,11... | collective-permute-start | bytes 1572872 | tf_op jit(solution)/shard_map/ppermute | solution.py:353
  2.2 9.1 %copy-start = (bf16[512,1,512]{2,0,1:T(8,128)(2,1)S(1)}, bf16[512,1,512]{2,0,1:T(8,128)(2,1)}, u32[]{:S(2)}) copy-start(bf16[512,1,512]{2,0,1:T(8,128)(2,1)} %param.5) | copy-start | bytes 1572868
  8.9 4.1 %collective-permute-start.2 = (bf16[512,512]{1,0:T(8,128)(2,1)S(1)}, bf16[512,512]{1,0:T(8,128)(2,1)S(1)}, u32[]{:S(2)}, u32[]{:S(2)}) collective-permute-start(bf16[512,512]{1,0:T(8,128)(2,1)S(1)} %collective-permute-done.refs_6_), channel_id=1, source_target_pairs={{0,1},{1,0},{2,3},{3,2},{4,5},{5,4},{6,7},{7,6},{8,9},{9,8},{10,11... | collective-permute-start | bytes 1572872 | tf_op jit(solution)/shard_map/ppermute | solution.py:360
  10.1 11.1 %collective-permute-start.3 = (bf16[512,512]{1,0:T(8,128)(2,1)S(1)}, bf16[512,512]{1,0:T(8,128)(2,1)S(1)}, u32[]{:S(2)}, u32[]{:S(2)}) collective-permute-start(bf16[512,512]{1,0:T(8,128)(2,1)S(1)} %collective-permute-done.refs_6_), channel_id=1, source_target_pairs={{0,4},{1,3},{2,6},{3,1},{4,0},{5,7},{6,2},{7,5},{8,10},{9,13},{10,... | collective-permute-start | bytes 1572872 | tf_op jit(solution)/shard_map/ppermute | solution.py:359
  11.3 9.9 %collective-permute-start.5 = (bf16[256,512]{1,0:T(8,128)(2,1)S(1)}, bf16[256,512]{1,0:T(8,128)(2,1)S(1)}, u32[]{:S(2)}, u32[]{:S(2)}) collective-permute-start(bf16[256,512]{1,0:T(8,128)(2,1)S(1)} %slice_bitcast_fusion), channel_id=1, source_target_pairs={{0,4},{1,3},{2,6},{3,1},{4,0},{5,7},{6,2},{7,5},{8,10},{9,13},{10,... | collective-permute-start | bytes 786440 | tf_op jit(solution)/shard_map/ppermute | solution.py:352
  11.6 9.6 %collective-permute-start.4 = (bf16[256,512]{1,0:T(8,128)(2,1)S(1)}, bf16[256,512]{1,0:T(8,128)(2,1)S(1)}, u32[]{:S(2)}, u32[]{:S(2)}) collective-permute-start(bf16[256,512]{1,0:T(8,128)(2,1)S(1)} %slice.9), channel_id=1, source_target_pairs={{0,8},{1,9},{2,10},{3,11},{4,12},{5,13},{6,14},{7,15},{8,0},{9,1},... | collective-permute-start | bytes 786440 | tf_op jit(solution)/shard_map/ppermute | solution.py:358
  21.2 3.2 %collective-permute-start.8 = (bf16[512,512]{1,0:T(8,128)(2,1)S(1)}, bf16[512,512]{1,0:T(8,128)(2,1)S(1)}, u32[]{:S(2)}, u32[]{:S(2)}) collective-permute-start(bf16[512,512]{1,0:T(8,128)(2,1)S(1)} %collective-permute-done.3.refs_2_), channel_id=1, source_target_pairs={{0,1},{1,0},{2,3},{3,2},{4,5},{5,4},{6,7},{7,6},{8,9},{9,8},{10,11... | collective-permute-start | bytes 1572872 | tf_op jit(solution)/shard_map/ppermute | solution.py:371
  22.1 1.9 %collective-permute-start.6 = (bf16[256,512]{1,0:T(8,128)(2,1)S(1)}, bf16[256,512]{1,0:T(8,128)(2,1)S(1)}, u32[]{:S(2)}, u32[]{:S(2)}) collective-permute-start(bf16[256,512]{1,0:T(8,128)(2,1)S(1)} %collective-permute-done.4.refs_0_), channel_id=1, source_target_pairs={{0,1},{1,0},{2,3},{3,2},{4,5},{5,4},{6,7},{7,6},{8,9},{9,8},{10,11... | collective-permute-start | bytes 786440 | tf_op jit(solution)/shard_map/ppermute | solution.py:369
  22.1 2.2 %collective-permute-start.7 = (bf16[256,512]{1,0:T(8,128)(2,1)S(1)}, bf16[256,512]{1,0:T(8,128)(2,1)S(1)}, u32[]{:S(2)}, u32[]{:S(2)}) collective-permute-start(bf16[256,512]{1,0:T(8,128)(2,1)S(1)} %collective-permute-done.5.refs_1_), channel_id=1, source_target_pairs={{0,1},{1,0},{2,3},{3,2},{4,5},{5,4},{6,7},{7,6},{8,9},{9,8},{10,11... | collective-permute-start | bytes 786440 | tf_op jit(solution)/shard_map/ppermute | solution.py:366
  26.3 4.8 %collective-permute-start.10 = (bf16[128,512]{1,0:T(8,128)(2,1)S(1)}, bf16[128,512]{1,0:T(8,128)(2,1)S(1)}, u32[]{:S(2)}, u32[]{:S(2)}) collective-permute-start(bf16[128,512]{1,0:T(8,128)(2,1)S(1)} %get-tuple-element.41), channel_id=1, source_target_pairs={{0,16},{8,24},{16,0},{24,8},{1,17},{9,25},{17,1},{25,9},{2,18},{10... | collective-permute-start | bytes 393224 | tf_op jit(solution)/shard_map/ppermute | solution.py:379
  26.6 10.0 %collective-permute-start.11 = (bf16[128,512]{1,0:T(8,128)(2,1)S(1)}, bf16[128,512]{1,0:T(8,128)(2,1)S(1)}, u32[]{:S(2)}, u32[]{:S(2)}) collective-permute-start(bf16[128,512]{1,0:T(8,128)(2,1)S(1)} %get-tuple-element.42), channel_id=1, source_target_pairs={{0,8},{8,0},{16,24},{24,16},{1,9},{9,1},{17,25},{25,17},{2,10},{10... | collective-permute-start | bytes 393224 | tf_op jit(solution)/shard_map/ppermute | solution.py:379
  29.9 11.2 %collective-permute-start.9 = (bf16[128,512]{1,0:T(8,128)(2,1)S(1)}, bf16[128,512]{1,0:T(8,128)(2,1)S(1)}, u32[]{:S(2)}, u32[]{:S(2)}) collective-permute-start(bf16[128,512]{1,0:T(8,128)(2,1)S(1)} %get-tuple-element.40), channel_id=1, source_target_pairs={{0,24},{8,16},{16,8},{24,0},{1,25},{9,17},{17,9},{25,1},{2,26},{10... | collective-permute-start | bytes 393224 | tf_op jit(solution)/shard_map/ppermute | solution.py:379
